TPU v7x, 32 devices: a whole 2x2x4 slice. The times are simulated.
32 devices in a mesh: azim: 8 (over y, x, core), axial: 4 (over z).
Axes of the slice: x: 2, y: 2, z: 4, core: 2. Of those that a mesh axis runs over, the one named last changes fastest.
Arguments:
- field: bfloat16 [2, 4, 128, 1024], P(None, None, 'axial', 'azim'), may hold values from -6 to 6
- near_tiles: bfloat16 [2, 16, 64, 2, 128, 128], P(None, 'axial', 'azim'), may hold values from -0.25 to 0.25
- near_pick: int32 [16, 64, 2], P('axial', 'azim'), may hold values from 0 to 48, all different within a row
- factors: bfloat16 [4, 8, 5, 4, 128, 128], P('axial', 'azim'), may hold values from -0.25 to 0.25
Outputs:
- scattered: float32 [2, 4, 128, 1024], P(None, None, 'axial', 'azim')
Inputs may be any that keep to these rules, and one draw needn't show every extreme that they name: `near_pick`: each tile names 2 different offsets within the square of 7**2 tile offsets.
All inputs are finite; a program needn't handle non-finite values.
Results may differ from a plain program's by a relative error of at most 0.0045.
Values may be sent and summed in bfloat16 or wider, within the bound.
A program may use at most 64 MiB of HBM per device.

v0:
```python
import functools

import jax
import jax.numpy as jnp
from jax import lax
from jax.experimental import pallas as pl
from jax.experimental.pallas import tpu as pltpu
from jax.sharding import PartitionSpec as P

TX = 8
TZ = 16
REACH = 3
SPAN = 2 * REACH + 1
F32 = jnp.float32
BF16 = jnp.bfloat16


def swap_groups(parts):
    lanes = len(parts) * TZ
    group = lax.broadcasted_iota(jnp.int32, parts[0].shape, 1) // TZ
    bit = len(parts) // 2
    while bit:
        high = (group & bit) != 0
        swapped = list(parts)
        for i in range(len(parts)):
            if i & bit == 0:
                low_part, high_part = parts[i], parts[i | bit]
                swapped[i] = jnp.where(high, pltpu.roll(high_part, bit * TZ, 1), low_part)
                swapped[i | bit] = jnp.where(
                    high, high_part, pltpu.roll(low_part, lanes - bit * TZ, 1)
                )
        parts = swapped
        bit //= 2
    return parts


def complex_fold(both, width):
    by_re, by_im = both[:, :width], both[:, width:]
    rows = both.shape[0]
    turned = pltpu.roll(by_im.reshape(rows // 8, 8, width), 4, 1).reshape(rows, width)
    row = lax.broadcasted_iota(jnp.int32, (rows, width), 0)
    return by_re + jnp.where((row & 4) == 0, -turned, turned)


def times(left, right):
    return lax.dot_general(
        left, right, (((1,), (1,)), ((), ())), preferred_element_type=F32
    )


def kernel(
    dims,
    pick_hbm,
    field_hbm,
    near_hbm,
    factors_hbm,
    out_ref,
    pick_ref,
    field_vm,
    wide,
    near_vm,
    weights,
    mate_weights,
    pad,
    near_sum,
    start,
    held,
    arrived,
    last,
    last_arrived,
    pick_sem,
    field_sem,
    near_sem,
    factor_sem,
    send_sem,
    recv_sem,
    mate_send,
    mate_recv,
    halo_send,
    halo_recv,
):
    azim_count, axial_count, plan, trows, tcols, lead, order = dims
    d = lax.axis_index("azim")
    e = lax.axis_index("axial")
    rows = trows * tcols * lead
    half = rows // 2

    def xor(value, bit):
        return value + (1 << bit) * (1 - 2 * ((value // (1 << bit)) % 2))

    partners = []
    for level, bit in enumerate(plan):
        if level < 3:
            partners.append({"azim": xor(d, bit), "axial": e})
        else:
            partners.append({"azim": d, "axial": xor(e, bit)})
    side = d % 2
    mate_d = xor(d, 0)
    mate = {"azim": mate_d, "axial": e}
    mine = pl.ds(pl.multiple_of(side * half, half), half)
    theirs = pl.ds(pl.multiple_of((1 - side) * half, half), half)
    cross = {"azim": xor(xor(d, plan[0]), 0), "axial": e}
    reached = sorted(1 << bit for bit in plan[:3]) == [1, 2, 4] and azim_count == 8
    right = (d + 1) % azim_count
    left = (d + azim_count - 1) % azim_count
    has_up = e > 0
    has_down = e < axial_count - 1

    barrier = pltpu.get_barrier_semaphore()

    def greet(device):
        pl.semaphore_signal(
            barrier, inc=1, device_id=device, device_id_type=pl.DeviceIdType.MESH
        )

    for partner in (partners[0], cross, partners[1], mate):
        greet(partner)
    if not reached:
        for column in (left, right):
            greet({"azim": column, "axial": e})

    @pl.when(has_up)
    def _():
        for column in (d,) if reached else (left, d, right):
            greet({"azim": column, "axial": e - 1})

    @pl.when(has_down)
    def _():
        for column in (d,) if reached else (left, d, right):
            greet({"azim": column, "axial": e + 1})

    field_copy = pltpu.make_async_copy(field_hbm, field_vm, field_sem)
    field_copy.start()
    factor_copy = pltpu.make_async_copy(factors_hbm.at[0, 0], weights, factor_sem)
    factor_copy.start()
    near_copies = [
        pltpu.make_async_copy(near_hbm.at[:, r], near_vm.at[:, r], near_sem.at[r])
        for r in range(trows)
    ]
    pick_copy = pltpu.make_async_copy(pick_hbm, pick_ref, pick_sem)
    pick_copy.start()
    for copy in near_copies:
        copy.start()

    @pl.when(jnp.logical_not(has_up))
    def _():
        pad[0:REACH] = jnp.zeros((REACH,) + pad.shape[1:], BF16)

    @pl.when(jnp.logical_not(has_down))
    def _():
        pad[REACH + trows :] = jnp.zeros((REACH,) + pad.shape[1:], BF16)

    field_copy.wait()
    wide[...] = field_vm[...].astype(F32)
    for r in range(trows):
        parts = [wide[pl.ds(r * TX + i, lead, stride=trows * TX), :] for i in range(TX)]
        tiles = swap_groups(parts)
        for c in range(tcols):
            pad[REACH + r, REACH + c] = tiles[c].astype(BF16)
        base = r * tcols * lead
        start[base : base + tcols * lead, :] = jnp.concatenate(tiles, axis=0).astype(BF16)

    edges = (e == 0).astype(jnp.int32) + (e == axial_count - 1).astype(jnp.int32)
    if reached:
        pl.semaphore_wait(barrier, 6 - edges)
    else:
        pl.semaphore_wait(barrier, 12 - 3 * edges)

    def remote(src, dst, sems, index, device):
        return pltpu.make_async_remote_copy(
            src_ref=src,
            dst_ref=dst,
            send_sem=sems[0].at[index],
            recv_sem=sems[1].at[index],
            device_id=device,
            device_id_type=pl.DeviceIdType.MESH,
        )

    pair_sems, mate_sems = (send_sem, recv_sem), (mate_send, mate_recv)
    axial_mate = {"azim": mate_d, "axial": partners[4]["axial"]}
    exchanges = {
        0: [
            remote(start.at[mine], arrived.at[0, 0], pair_sems, (0, 0), partners[0]),
            remote(start.at[theirs], arrived.at[0, 1], pair_sems, (0, 1), cross),
        ],
        4: [
            remote(last.at[mine], last_arrived.at[mine], pair_sems, (4, 0), partners[4]),
            remote(held.at[4, 1], last_arrived.at[mine], pair_sems, (4, 1), axial_mate),
        ],
    }
    for level in (1, 3):
        exchanges[level] = [
            remote(
                held.at[level, role],
                arrived.at[level, role],
                pair_sems,
                (level, role),
                partners[level],
            )
            for role in range(2)
        ]
    first_half = remote(start.at[theirs], held.at[0, 1], mate_sems, 0, mate)
    last_half = remote(held.at[4, 1], last.at[mine], mate_sems, 1, mate)
    factor_sends = [
        remote(weights.at[level], mate_weights.at[level], mate_sems, 2 + level, mate)
        for level in range(len(plan) - 1)
    ]

    for copy in exchanges[0]:
        copy.start()
    first_half.start()
    factor_copy.wait()
    for copy in factor_sends:
        copy.start()

    def halo(index, src_rows, src_cols, dst_row, dst_col, device):
        count_r, count_c = src_rows[1] - src_rows[0], src_cols[1] - src_cols[0]
        return pltpu.make_async_remote_copy(
            src_ref=pad.at[
                pl.ds(REACH + src_rows[0], count_r), pl.ds(REACH + src_cols[0], count_c)
            ],
            dst_ref=pad.at[pl.ds(dst_row, count_r), pl.ds(dst_col, count_c)],
            send_sem=halo_send.at[index],
            recv_sem=halo_recv.at[index],
            device_id=device,
            device_id_type=pl.DeviceIdType.MESH,
        )

    every_r, every_c = (0, trows), (0, tcols)
    head_r, head_c = (0, REACH), (0, REACH)
    tail_r, tail_c = (trows - REACH, trows), (tcols - REACH, tcols)
    past_r, past_c = REACH + trows, REACH + tcols
    level_halos = [
        halo(0, every_r, tail_c, REACH, 0, {"azim": right, "axial": e}),
        halo(1, every_r, head_c, REACH, past_c, {"azim": left, "axial": e}),
    ]
    down_halos = [
        halo(2, tail_r, every_c, 0, REACH, {"azim": d, "axial": e + 1}),
        halo(3, tail_r, tail_c, 0, 0, {"azim": right, "axial": e + 1}),
        halo(4, tail_r, head_c, 0, past_c, {"azim": left, "axial": e + 1}),
    ]
    up_halos = [
        halo(5, head_r, every_c, past_r, REACH, {"azim": d, "axial": e - 1}),
        halo(6, head_r, tail_c, past_r, 0, {"azim": right, "axial": e - 1}),
        halo(7, head_r, head_c, past_r, past_c, {"azim": left, "axial": e - 1}),
    ]

    @pl.when(has_down)
    def _():
        down_halos[0].start()

    @pl.when(has_up)
    def _():
        up_halos[0].start()

    def corner_halos():
        @pl.when(has_down)
        def _():
            for copy in down_halos[1:]:
                copy.start()

        @pl.when(has_up)
        def _():
            for copy in up_halos[1:]:
                copy.start()

    def met_axial():
        @pl.when(has_up)
        def _():
            down_halos[0].wait_recv()

        @pl.when(has_down)
        def _():
            up_halos[0].wait_recv()

    def near_field():
        @pl.when(has_up)
        def _():
            for copy in down_halos[1:]:
                copy.wait_recv()

        @pl.when(has_down)
        def _():
            for copy in up_halos[1:]:
                copy.wait_recv()

        for copy in level_halos:
            copy.wait_recv()
        pick_copy.wait()
        for copy in near_copies:
            copy.wait()

        width = near_vm.shape[-1]

        def tile_row(r, carry):
            for c in range(tcols):
                sources = []
                for k in range(near_vm.shape[3]):
                    offset = pick_ref[r, k, c]
                    row = r + lax.div(offset, SPAN)
                    column = c + lax.rem(offset, SPAN)
                    sources.append(pad[row, column])
                blocks = jnp.concatenate(
                    [
                        near_vm[:, r, c, k].reshape(2 * width, width)
                        for k in range(near_vm.shape[3])
                    ],
                    axis=1,
                )
                both = times(jnp.concatenate(sources, axis=1), blocks)
                at = pl.multiple_of((r * tcols + c) * lead, lead)
                near_sum[pl.ds(at, lead), :] = complex_fold(both, width)
            return carry

        lax.fori_loop(0, trows, tile_row, 0)

    width = weights.shape[-1]
    by_role = (weights, mate_weights)

    def block(ref, level, which):
        return ref[level, 2 * which : 2 * which + 2].reshape(2 * width, width)

    def joined(own, level, role):
        both = own + times(arrived[level, role], block(by_role[role], level, 1))
        return complex_fold(both, width)

    own = [times(start[mine, :], block(weights, 0, 0))]
    first_half.wait_recv()
    factor_sends[0].wait_recv()
    own.append(times(held[0, 1], block(mate_weights, 0, 0)))
    for role in range(2):
        exchanges[0][role].wait_recv()
        held[1, role] = joined(own[role], 0, role).astype(BF16)
        exchanges[1][role].start()
    factor_sends[1].wait_recv()
    own = [times(held[1, role], block(by_role[role], 1, 0)) for role in range(2)]
    factor_sends[2].wait_recv()
    met_axial()
    for copy in exchanges[1]:
        copy.wait_recv()
    coeffs = [joined(own[role], 1, role).astype(BF16) for role in range(2)]

    for role in range(2):
        both = times(coeffs[role], block(by_role[role], 2, 0)) + times(
            coeffs[1 - role], block(by_role[role], 2, 1)
        )
        held[3, role] = complex_fold(both, width).astype(BF16)
        exchanges[3][role].start()
    for copy in level_halos:
        copy.start()
    corner_halos()

    factor_sends[3].wait_recv()
    own = [times(held[3, role], block(by_role[role], 3, 0)) for role in range(2)]
    exchanges[3][0].wait_recv()
    last[mine, :] = joined(own[0], 3, 0).astype(BF16)
    exchanges[4][0].start()
    exchanges[3][1].wait_recv()
    held[4, 1] = joined(own[1], 3, 1).astype(BF16)
    exchanges[4][1].start()
    last_half.start()

    near_field()
    near_sum[mine, :] += complex_fold(times(last[mine, :], block(weights, 4, 0)), width)
    last_half.wait_recv()
    near_sum[theirs, :] += complex_fold(times(last[theirs, :], block(weights, 4, 0)), width)
    for copy in exchanges[4]:
        copy.wait_recv()
    per = tcols * lead
    for j, part in enumerate((mine, theirs)):
        both = times(last_arrived[part, :], block(weights, 4, 1))
        total = complex_fold(both, width) + near_sum[part, :]
        first = (side if j == 0 else 1 - side) * (half // per)
        for q in range(half // per):
            parts = swap_groups(
                [
                    total[q * per + c * lead : q * per + (c + 1) * lead]
                    for c in range(tcols)
                ]
            )
            for i in range(TX):
                at = (first + q) * TX + i
                out_ref[pl.ds(at, lead, stride=trows * TX), :] = parts[i]

    for copies in exchanges.values():
        for copy in copies:
            copy.wait_send()
    for copy in [first_half, last_half] + factor_sends:
        copy.wait_send()

    @pl.when(has_down)
    def _():
        for copy in down_halos:
            copy.wait_send()

    @pl.when(has_up)
    def _():
        for copy in up_halos:
            copy.wait_send()

    for copy in level_halos:
        copy.wait_send()


def solution(mesh):
    placed = (
        P(None, None, "axial", "azim"),
        P(None, "axial", "azim", None, None, None),
        P("axial", "azim", None),
        P("axial", "azim", None, None, None, None),
    )
    azim_count, axial_count = mesh.shape["azim"], mesh.shape["axial"]
    top = azim_count.bit_length() - 1
    plan = (top - 1, top - 2, 0, 1, 0)

    def on_device(field, near_tiles, near_pick, factors):
        parts, angles, rows, columns = field.shape
        lead = parts * angles
        trows, tcols = rows // TX, columns // TZ
        cells = TX * TZ
        flat = field.reshape(lead * rows, columns)
        total = trows * tcols * lead
        dims = (azim_count, axial_count, plan, trows, tcols, lead, tuple(mesh.axis_names))
        any_space = pl.BlockSpec(memory_space=pl.ANY)
        out = pl.pallas_call(
            functools.partial(kernel, dims),
            out_shape=pltpu.VMEM((lead * rows, columns), F32),
            in_specs=[any_space] * 4,
            out_specs=pl.BlockSpec(memory_space=pltpu.VMEM),
            scratch_shapes=[
                pltpu.SMEM((trows, near_pick.shape[2], tcols), jnp.int32),
                pltpu.VMEM(flat.shape, BF16),
                pltpu.VMEM(flat.shape, F32),
                pltpu.VMEM(near_tiles.shape, BF16),
                pltpu.VMEM(factors.shape[2:], BF16),
                pltpu.VMEM(factors.shape[2:], BF16),
                pltpu.VMEM((trows + 2 * REACH, tcols + 2 * REACH, lead, cells), BF16),
                pltpu.VMEM((total, cells), F32),
                pltpu.VMEM((total, cells), BF16),
                pltpu.VMEM((len(plan), 2, total // 2, cells), BF16),
                pltpu.VMEM((len(plan), 2, total // 2, cells), BF16),
                pltpu.VMEM((total, cells), BF16),
                pltpu.VMEM((total, cells), BF16),
                pltpu.SemaphoreType.DMA,
                pltpu.SemaphoreType.DMA,
                pltpu.SemaphoreType.DMA((trows,)),
                pltpu.SemaphoreType.DMA,
                pltpu.SemaphoreType.DMA((len(plan), 2)),
                pltpu.SemaphoreType.DMA((len(plan), 2)),
                pltpu.SemaphoreType.DMA((len(plan) + 1,)),
                pltpu.SemaphoreType.DMA((len(plan) + 1,)),
                pltpu.SemaphoreType.DMA((8,)),
                pltpu.SemaphoreType.DMA((8,)),
            ],
            compiler_params=pltpu.CompilerParams(collective_id=0, has_side_effects=True),
        )(near_pick.transpose(0, 2, 1), flat, near_tiles, factors)
        return out.reshape(field.shape)

    return jax.shard_map(
        on_device,
        mesh=mesh,
        in_specs=placed,
        out_specs=P(None, None, "axial", "azim"),
        check_vma=False,
    )
```

profile of v0, /device:TPU:0, one launch (start us, length us, event | category | flops | bytes accessed | tf_op | source)
XLA Modules:
  0.0 21.3 jit_solution(5050938535298075057)
XLA Ops:
  0.0 20.6 %shard_map.46 = f32[256,128]{1,0:T(8,128)S(1)} custom-call(s32[4,2,8]{2,1,0:T(2,128)} %bitcast.5, bf16[256,128]{1,0:T(8,128)(2,1)} %bitcast.4, bf16[2,4,8,2,128,128]{5,4,3,2,1,0:T(8,128)(2,1)} %near_hbm.1, bf16[1,1,5,4,128,128]{5,4,3,2,1,0:T(8,128)(2,1)} %factors_hbm.1), custom_call_target="tpu_custom_call" | custom-call | tf_op jit(solution)/shard_map/pallas_call | solution.py:425
  20.6 0.7 %copy.6 = f32[2,4,32,128]{3,2,1,0:T(8,128)} copy(f32[2,4,32,128]{3,2,1,0:T(8,128)S(1)} %bitcast.3) | data formatting | bytes 262144
where the time goes:
time: 21.4 us; the launch traced here: 21.3 us
  Pallas kernels  20.6 us (96%)
  local copies, waits for them, and re-layouts  0.66 us (3%)
    pallas_call x1, Pallas kernels, on_device(): pl.pallas_call(functools.partial(kernel, dims), out_shape=pltpu.VMEM((lea...  20.6 us
    unnamed x1, local copies, waits for them, and re-layouts  0.66 us

commit v1 on v0

--- a/solution.py
+++ b/solution.py
@@ -121,13 +121,11 @@
 
     @pl.when(has_up)
     def _():
-        for column in (d,) if reached else (left, d, right):
-            greet({"azim": column, "axial": e - 1})
+        greet({"azim": d, "axial": e - 1})
 
     @pl.when(has_down)
     def _():
-        for column in (d,) if reached else (left, d, right):
-            greet({"azim": column, "axial": e + 1})
+        greet({"azim": d, "axial": e + 1})
 
     field_copy = pltpu.make_async_copy(field_hbm, field_vm, field_sem)
     field_copy.start()
@@ -139,16 +137,16 @@
     ]
     pick_copy = pltpu.make_async_copy(pick_hbm, pick_ref, pick_sem)
     pick_copy.start()
-    for copy in near_copies:
-        copy.start()
+
+    own_c = slice(REACH, REACH + tcols)
 
     @pl.when(jnp.logical_not(has_up))
     def _():
-        pad[0:REACH] = jnp.zeros((REACH,) + pad.shape[1:], BF16)
+        pad[0:REACH, own_c] = jnp.zeros((REACH, tcols) + pad.shape[2:], BF16)
 
     @pl.when(jnp.logical_not(has_down))
     def _():
-        pad[REACH + trows :] = jnp.zeros((REACH,) + pad.shape[1:], BF16)
+        pad[REACH + trows :, own_c] = jnp.zeros((REACH, tcols) + pad.shape[2:], BF16)
 
     field_copy.wait()
     wide[...] = field_vm[...].astype(F32)
@@ -164,7 +162,7 @@
     if reached:
         pl.semaphore_wait(barrier, 6 - edges)
     else:
-        pl.semaphore_wait(barrier, 12 - 3 * edges)
+        pl.semaphore_wait(barrier, 8 - edges)
 
     def remote(src, dst, sems, index, device):
         return pltpu.make_async_remote_copy(
@@ -212,6 +210,8 @@
     factor_copy.wait()
     for copy in factor_sends:
         copy.start()
+    for copy in near_copies:
+        copy.start()
 
     def halo(index, src_rows, src_cols, dst_row, dst_col, device):
         count_r, count_c = src_rows[1] - src_rows[0], src_cols[1] - src_cols[0]
@@ -226,64 +226,35 @@
             device_id_type=pl.DeviceIdType.MESH,
         )
 
-    every_r, every_c = (0, trows), (0, tcols)
-    head_r, head_c = (0, REACH), (0, REACH)
-    tail_r, tail_c = (trows - REACH, trows), (tcols - REACH, tcols)
+    every_c = (0, tcols)
+    whole_r = (-REACH, trows + REACH)
+    head_c, tail_c = (0, REACH), (tcols - REACH, tcols)
     past_r, past_c = REACH + trows, REACH + tcols
     level_halos = [
-        halo(0, every_r, tail_c, REACH, 0, {"azim": right, "axial": e}),
-        halo(1, every_r, head_c, REACH, past_c, {"azim": left, "axial": e}),
+        halo(0, whole_r, tail_c, 0, 0, {"azim": right, "axial": e}),
+        halo(1, whole_r, head_c, 0, past_c, {"azim": left, "axial": e}),
     ]
-    down_halos = [
-        halo(2, tail_r, every_c, 0, REACH, {"azim": d, "axial": e + 1}),
-        halo(3, tail_r, tail_c, 0, 0, {"azim": right, "axial": e + 1}),
-        halo(4, tail_r, head_c, 0, past_c, {"azim": left, "axial": e + 1}),
-    ]
-    up_halos = [
-        halo(5, head_r, every_c, past_r, REACH, {"azim": d, "axial": e - 1}),
-        halo(6, head_r, tail_c, past_r, 0, {"azim": right, "axial": e - 1}),
-        halo(7, head_r, head_c, past_r, past_c, {"azim": left, "axial": e - 1}),
-    ]
+    down_halo = halo(2, (trows - REACH, trows), every_c, 0, REACH, {"azim": d, "axial": e + 1})
+    up_halo = halo(3, (0, REACH), every_c, past_r, REACH, {"azim": d, "axial": e - 1})
 
     @pl.when(has_down)
     def _():
-        down_halos[0].start()
+        down_halo.start()
 
     @pl.when(has_up)
     def _():
-        up_halos[0].start()
-
-    def corner_halos():
-        @pl.when(has_down)
-        def _():
-            for copy in down_halos[1:]:
-                copy.start()
-
-        @pl.when(has_up)
-        def _():
-            for copy in up_halos[1:]:
-                copy.start()
+        up_halo.start()
 
     def met_axial():
         @pl.when(has_up)
         def _():
-            down_halos[0].wait_recv()
+            down_halo.wait_recv()
 
         @pl.when(has_down)
         def _():
-            up_halos[0].wait_recv()
+            up_halo.wait_recv()
 
     def near_field():
-        @pl.when(has_up)
-        def _():
-            for copy in down_halos[1:]:
-                copy.wait_recv()
-
-        @pl.when(has_down)
-        def _():
-            for copy in up_halos[1:]:
-                copy.wait_recv()
-
         for copy in level_halos:
             copy.wait_recv()
         pick_copy.wait()
@@ -348,7 +319,6 @@
         exchanges[3][role].start()
     for copy in level_halos:
         copy.start()
-    corner_halos()
 
     factor_sends[3].wait_recv()
     own = [times(held[3, role], block(by_role[role], 3, 0)) for role in range(2)]
@@ -390,13 +360,11 @@
 
     @pl.when(has_down)
     def _():
-        for copy in down_halos:
-            copy.wait_send()
+        down_halo.wait_send()
 
     @pl.when(has_up)
     def _():
-        for copy in up_halos:
-            copy.wait_send()
+        up_halo.wait_send()
 
     for copy in level_halos:
         copy.wait_send()
@@ -449,8 +417,8 @@
                 pltpu.SemaphoreType.DMA((len(plan), 2)),
                 pltpu.SemaphoreType.DMA((len(plan) + 1,)),
                 pltpu.SemaphoreType.DMA((len(plan) + 1,)),
-                pltpu.SemaphoreType.DMA((8,)),
-                pltpu.SemaphoreType.DMA((8,)),
+                pltpu.SemaphoreType.DMA((4,)),
+                pltpu.SemaphoreType.DMA((4,)),
             ],
             compiler_params=pltpu.CompilerParams(collective_id=0, has_side_effects=True),
         )(near_pick.transpose(0, 2, 1), flat, near_tiles, factors)

time: 21.4 us -> 20.3 us (0.949)
  Pallas kernels: 20.6 us -> 19.5 us
    pallas_call x1, Pallas kernels: 20.6 us -> 19.5 us  [on_device(): pl.pallas_call(functools.partial(kernel, dims), out_shape=pltpu.VMEM((lea...]
where the time goes in v1:
time: 20.3 us; the launch traced here: 20.2 us
  Pallas kernels  19.5 us (96%)
  local copies, waits for them, and re-layouts  0.66 us (3%)
    pallas_call x1, Pallas kernels, on_device(): pl.pallas_call(functools.partial(kernel, dims), out_shape=pltpu.VMEM((lea...  19.5 us
    unnamed x1, local copies, waits for them, and re-layouts  0.66 us

profile of v1, /device:TPU:0, one launch (start us, length us, event | category | flops | bytes accessed | tf_op | source)
XLA Modules:
  0.0 20.2 jit_solution(14426073120646123538)
XLA Ops:
  0.0 19.5 %shard_map.46 = f32[256,128]{1,0:T(8,128)S(1)} custom-call(s32[4,2,8]{2,1,0:T(2,128)} %bitcast.5, bf16[256,128]{1,0:T(8,128)(2,1)} %bitcast.4, bf16[2,4,8,2,128,128]{5,4,3,2,1,0:T(8,128)(2,1)} %near_hbm.1, bf16[1,1,5,4,128,128]{5,4,3,2,1,0:T(8,128)(2,1)} %factors_hbm.1), custom_call_target="tpu_custom_call" | custom-call | tf_op jit(solution)/shard_map/pallas_call | solution.py:393
  19.5 0.7 %copy.6 = f32[2,4,32,128]{3,2,1,0:T(8,128)} copy(f32[2,4,32,128]{3,2,1,0:T(8,128)S(1)} %bitcast.3) | data formatting | bytes 262144
